TPU v7x, 32 devices: a whole 2x2x4 slice. The times are simulated.
32 devices in a mesh: shard: 4 (over z), ctx: 2 (over x), tp: 4 (over y, core).
Axes of the slice: x: 2, y: 2, z: 4, core: 2. Of those that a mesh axis runs over, the one named last changes fastest.
Arguments:
- activations: bfloat16 [4, 1040, 768], P('shard', 'ctx'), may hold values from -6 to 6
- slot_counts: int32 [4, 2], P('shard'), may hold values from 1 to 520, as said below
- qkv_weight: bfloat16 [3, 768, 768], P(None, 'shard', 'tp'), may hold values from -0.21875 to 0.21875
- proj_weight: bfloat16 [768, 768], P('tp', 'shard'), may hold values from -3 to 3
- up_weight: bfloat16 [768, 3072], P('shard', 'tp'), may hold values from -0.21875 to 0.21875
- down_weight: bfloat16 [3072, 768], P('tp', 'shard'), may hold values from -0.109375 to 0.109375
- norm_gains: bfloat16 [2, 768], P(None, 'shard'), may hold values from 0.5 to 1.5
- row_biases: bfloat16 [4, 768], P(None, 'shard'), may hold values from -3 to 3
- head_biases: bfloat16 [2, 768], P(None, 'tp'), may hold values from -0.59765625 to 0.59765625
- hidden_bias: bfloat16 [3072], P('tp'), may hold values from -3 to 3
- cotangent: bfloat16 [4, 1040, 768], P('shard', 'ctx'), may hold values from -6 to 6
Outputs:
- layer_out: bfloat16 [4, 1040, 768], P('shard', ('ctx', 'tp'))
- input_grad: bfloat16 [4, 1040, 768], P('shard', ('ctx', 'tp'))
- qkv_weight_grad: float32 [3, 768, 768], P(None, 'shard', 'tp')
- proj_weight_grad: float32 [768, 768], P('tp', 'shard')
- up_weight_grad: float32 [768, 3072], P('shard', 'tp')
- down_weight_grad: float32 [3072, 768], P('tp', 'shard')
- norm_gains_grad: float32 [2, 768], P(None, 'shard')
- row_biases_grad: float32 [4, 768], P(None, 'shard')
- head_biases_grad: float32 [2, 768], P(None, 'tp')
- hidden_bias_grad: float32 [3072], P('tp')
Inputs may be any that keep to these rules, and one draw needn't show every extreme that they name: Row b splits image b's 1025 tokens over the indices of ctx: slot_counts[b, r] of them lie in the first slots of index r's 520; each row sums to 1025; in each row one index holds exactly 520 and the others share the rest as evenly as possible.
All inputs are finite; a program needn't handle non-finite values.
Results may differ from a plain program's by a relative error of at most 0.012.
Values may be sent and summed in bfloat16 or wider, within the bound.
No kernel may reach another device: no remote copies, remote signals or barrier semaphores. Data moves between devices by JAX's collectives and lax.ppermute only.
A program may use at most 64 MiB of HBM per device.

v0:
```python
import math
import jax
import jax.numpy as jnp
from jax import lax
from jax.sharding import PartitionSpec as P

HD = 64
EPS = 1e-06
NEG = -1e30


def layer_norm(values, gain, shift):
    centred = values - jnp.mean(values, axis=-1, keepdims=True)
    spread = jnp.mean(centred * centred, axis=-1, keepdims=True)
    return centred * lax.rsqrt(spread + EPS) * gain + shift


def exact_gelu(hidden):
    return jax.nn.gelu(hidden, approximate=False)


def head_scores(queries, keys, keep):
    scale = 1.0 / math.sqrt(HD)
    scores = jnp.einsum("qhd,khd->hqk", queries, keys, preferred_element_type=jnp.float32) * scale
    return jnp.where(keep[None, None, :], scores, NEG)


def attend(item):
    queries, keys, values, keep = item
    slot_total = queries.shape[0]
    query_heads = queries.reshape(slot_total, -1, HD)
    key_heads = keys.reshape(keys.shape[0], -1, HD)
    value_heads = values.reshape(values.shape[0], -1, HD)
    scores = head_scores(query_heads, key_heads, keep)
    peak = jnp.max(scores, axis=-1, keepdims=True)
    log_total = peak + jnp.log(jnp.sum(jnp.exp(scores - peak), axis=-1, keepdims=True))
    attn_weights = jnp.exp(scores - log_total).astype(jnp.bfloat16)
    mixed = jnp.einsum(
        "hqk,khd->qhd", attn_weights, value_heads, preferred_element_type=jnp.float32
    )
    return (mixed.reshape(slot_total, -1).astype(jnp.bfloat16), log_total)


def attend_back(item):
    queries, keys, values, keep, log_total, grad_mixed = item
    scale = 1.0 / math.sqrt(HD)
    slot_total = queries.shape[0]
    key_total = keys.shape[0]
    query_heads = queries.reshape(slot_total, -1, HD)
    key_heads = keys.reshape(key_total, -1, HD)
    value_heads = values.reshape(key_total, -1, HD)
    grad_heads = grad_mixed.reshape(slot_total, -1, HD)
    scores = head_scores(query_heads, key_heads, keep)
    attn_weights = jnp.exp(scores - log_total)
    weights_low = attn_weights.astype(jnp.bfloat16)
    grad_weights = jnp.einsum(
        "qhd,khd->hqk", grad_heads, value_heads, preferred_element_type=jnp.float32
    )
    grad_values = jnp.einsum(
        "hqk,qhd->khd", weights_low, grad_heads, preferred_element_type=jnp.float32
    )
    inner = jnp.sum(grad_weights * attn_weights, axis=-1, keepdims=True)
    grad_scores = (attn_weights * (grad_weights - inner)).astype(jnp.bfloat16)
    grad_queries = (
        jnp.einsum("hqk,khd->qhd", grad_scores, key_heads, preferred_element_type=jnp.float32)
        * scale
    )
    grad_keys = (
        jnp.einsum("hqk,qhd->khd", grad_scores, query_heads, preferred_element_type=jnp.float32)
        * scale
    )
    return (
        grad_queries.reshape(slot_total, -1),
        grad_keys.reshape(key_total, -1),
        grad_values.reshape(key_total, -1),
    )


def per_device(
    activations,
    slot_counts,
    qkv_weight,
    proj_weight,
    up_weight,
    down_weight,
    norm_gains,
    row_biases,
    head_biases,
    hidden_bias,
    cotangent,
):
    images, slots, width = activations.shape
    n_ctx = lax.axis_size("ctx")
    n_tp = lax.axis_size("tp")
    row_count = images * slots
    quarter = row_count // n_tp
    row_start = lax.axis_index("tp") * quarter

    def own_rows(values):
        return lax.dynamic_slice_in_dim(values, row_start, quarter, 0)

    gathered = (
        lax.all_gather(qkv_weight, "shard", axis=1, tiled=True),
        lax.all_gather(proj_weight, "shard", axis=1, tiled=True),
        lax.all_gather(up_weight, "shard", axis=0, tiled=True),
        lax.all_gather(down_weight, "shard", axis=1, tiled=True),
        lax.all_gather(norm_gains, "shard", axis=1, tiled=True),
        lax.all_gather(row_biases, "shard", axis=1, tiled=True),
    )
    qkv_full, proj_full, up_full, down_full, gains_full, shifts_full = gathered
    gains = gains_full.astype(jnp.float32)
    shifts = shifts_full.astype(jnp.float32)
    ctx_rank = lax.axis_index("ctx")
    rank_ids = jnp.arange(n_ctx, dtype=jnp.int32)
    own_count = jnp.sum(jnp.where(rank_ids[None, :] == ctx_rank, slot_counts, 0), axis=1)
    slot_ids = jnp.arange(slots, dtype=jnp.int32)
    row_valid = (slot_ids[None, :] < own_count[:, None]).reshape(row_count, 1)
    share_valid = own_rows(row_valid)
    key_valid = jnp.repeat(slot_counts, slots, axis=1) > jnp.tile(slot_ids, n_ctx)[None, :]
    act_in = activations.reshape(row_count, width).astype(jnp.float32)
    normed, norm_one_back = jax.vjp(layer_norm, act_in, gains[0], shifts[0])
    normed_low = normed.astype(jnp.bfloat16)
    projected = jnp.einsum("rd,kde->kre", normed_low, qkv_full, preferred_element_type=jnp.float32)
    biases = head_biases.astype(jnp.float32)
    queries = (projected[0] + biases[0]).astype(jnp.bfloat16).reshape(images, slots, -1)
    keys = projected[1].astype(jnp.bfloat16).reshape(images, slots, -1)
    values = (projected[2] + biases[1]).astype(jnp.bfloat16).reshape(images, slots, -1)
    keys_all, values_all = (
        lax.all_gather(keys, "ctx", axis=1, tiled=True),
        lax.all_gather(values, "ctx", axis=1, tiled=True),
    )
    mixed, log_totals = lax.map(attend, (queries, keys_all, values_all, key_valid))
    mixed_flat = mixed.reshape(row_count, -1)
    attn_part = jnp.dot(mixed_flat, proj_full, preferred_element_type=jnp.float32)
    attn_sum = lax.psum(attn_part, "tp")
    middle_full = act_in + attn_sum + shifts[2]
    normed_two, norm_two_back = jax.vjp(layer_norm, middle_full, gains[1], shifts[1])
    normed_two_low = normed_two.astype(jnp.bfloat16)
    middle = own_rows(middle_full)
    hidden = jnp.dot(
        normed_two_low, up_full, preferred_element_type=jnp.float32
    ) + hidden_bias.astype(jnp.float32)
    gelu_out, gelu_back = jax.vjp(exact_gelu, hidden)
    gelu_low = gelu_out.astype(jnp.bfloat16)
    mlp_part = jnp.dot(gelu_low, down_full, preferred_element_type=jnp.float32)
    mlp_sum = own_rows(lax.psum(mlp_part.astype(jnp.bfloat16), "tp").astype(jnp.float32))
    layer_out = (
        jnp.where(share_valid, middle + mlp_sum + shifts[3], 0.0)
        .astype(jnp.bfloat16)
        .reshape(images, quarter, width)
    )
    qkv_use, proj_use, up_use, down_use = (qkv_full, proj_full, up_full, down_full)
    grad_out = jnp.where(row_valid, cotangent.reshape(row_count, width).astype(jnp.float32), 0.0)
    grad_branch = grad_out.astype(jnp.bfloat16)
    down_grad = jnp.einsum("rf,rd->fd", gelu_low, grad_branch, preferred_element_type=jnp.float32)
    grad_gelu = jnp.einsum("rd,fd->rf", grad_branch, down_use, preferred_element_type=jnp.float32)
    (grad_hidden,) = gelu_back(grad_gelu)
    grad_hidden_low = grad_hidden.astype(jnp.bfloat16)
    up_grad = jnp.einsum(
        "rd,rf->df", normed_two_low, grad_hidden_low, preferred_element_type=jnp.float32
    )
    hidden_grad = jnp.sum(grad_hidden_low.astype(jnp.float32), axis=0)
    grad_normed_part = jnp.einsum(
        "rf,df->rd", grad_hidden_low, up_use, preferred_element_type=jnp.float32
    )
    grad_normed_two = lax.psum(grad_normed_part, "tp")
    grad_middle_norm, gain_two_grad, shift_two_grad = norm_two_back(grad_normed_two)
    grad_middle_full = grad_out + grad_middle_norm
    grad_attn = grad_middle_full.astype(jnp.bfloat16)
    grad_middle = own_rows(grad_middle_full)
    proj_grad = jnp.einsum("re,rd->ed", mixed_flat, grad_attn, preferred_element_type=jnp.float32)
    grad_mixed = (
        jnp.einsum("rd,ed->re", grad_attn, proj_use, preferred_element_type=jnp.float32)
        .astype(jnp.bfloat16)
        .reshape(images, slots, -1)
    )
    grad_queries, grad_keys_part, grad_values_part = lax.map(
        attend_back, (queries, keys_all, values_all, key_valid, log_totals, grad_mixed)
    )
    grad_keys, grad_values = (
        lax.psum_scatter(grad_keys_part, "ctx", scatter_dimension=1, tiled=True),
        lax.psum_scatter(grad_values_part, "ctx", scatter_dimension=1, tiled=True),
    )
    stacked = jnp.stack(
        [
            grad_queries.reshape(row_count, -1),
            grad_keys.reshape(row_count, -1),
            grad_values.reshape(row_count, -1),
        ]
    ).astype(jnp.bfloat16)
    qkv_grad = jnp.einsum("rd,kre->kde", normed_low, stacked, preferred_element_type=jnp.float32)
    stacked_wide = stacked.astype(jnp.float32)
    head_grad = jnp.stack([jnp.sum(stacked_wide[0], axis=0), jnp.sum(stacked_wide[2], axis=0)])
    grad_normed_one_part = jnp.einsum(
        "kre,kde->rd", stacked, qkv_use, preferred_element_type=jnp.float32
    )
    grad_normed_one = lax.psum(grad_normed_one_part, "tp")
    grad_input_norm_full, gain_one_grad, shift_one_grad = norm_one_back(grad_normed_one)
    grad_input_norm = own_rows(grad_input_norm_full)
    gains_grad = jnp.stack([gain_one_grad, gain_two_grad])
    norm_shift_grads = jnp.stack([shift_one_grad, shift_two_grad])
    input_grad = (
        (grad_middle + grad_input_norm).astype(jnp.bfloat16).reshape(images, quarter, width)
    )
    shifts_grad = jnp.concatenate(
        [
            norm_shift_grads,
            jnp.stack(
                [
                    jnp.sum(grad_attn.astype(jnp.float32), axis=0),
                    jnp.sum(grad_branch.astype(jnp.float32), axis=0),
                ]
            ),
        ],
        axis=0,
    )
    summed = lax.psum((qkv_grad, proj_grad, up_grad, down_grad, gains_grad, shifts_grad), "ctx")
    owned = (
        lax.psum_scatter(summed[0], "shard", scatter_dimension=1, tiled=True),
        lax.psum_scatter(summed[1], "shard", scatter_dimension=1, tiled=True),
        lax.psum_scatter(summed[2], "shard", scatter_dimension=0, tiled=True),
        lax.psum_scatter(summed[3], "shard", scatter_dimension=1, tiled=True),
        lax.psum_scatter(summed[4], "shard", scatter_dimension=1, tiled=True),
        lax.psum_scatter(summed[5], "shard", scatter_dimension=1, tiled=True),
    )
    bias_totals = lax.psum((head_grad, hidden_grad), ("shard", "ctx"))
    return (
        layer_out,
        input_grad,
        owned[0],
        owned[1],
        owned[2],
        owned[3],
        owned[4],
        owned[5],
        bias_totals[0],
        bias_totals[1],
    )


def solution(mesh):
    placed = (
        P("shard", "ctx", None),
        P("shard", None),
        P(None, "shard", "tp"),
        P("tp", "shard"),
        P("shard", "tp"),
        P("tp", "shard"),
        P(None, "shard"),
        P(None, "shard"),
        P(None, "tp"),
        P("tp"),
        P("shard", "ctx", None),
    )
    return jax.shard_map(
        per_device,
        mesh=mesh,
        in_specs=placed,
        out_specs=(
            P("shard", ("ctx", "tp"), None),
            P("shard", ("ctx", "tp"), None),
            P(None, "shard", "tp"),
            P("tp", "shard"),
            P("shard", "tp"),
            P("tp", "shard"),
            P(None, "shard"),
            P(None, "shard"),
            P(None, "tp"),
            P("tp"),
        ),
        check_vma=False,
    )
```

profile of v0, /device:TPU:0, one launch (start us, length us, event | category | flops | bytes accessed | tf_op | source)
XLA Modules:
  0.0 542.7 jit_solution(16820646463041530862)
XLA Ops:
  10.4 12.8 %all-gather = bf16[4,192,2]{1,2,0:T(2,128)(2,1)S(1)} all-gather(bf16[1,192,2]{1,2,0:T(2,128)(2,1)} %bitcast.183), channel_id=1, replica_groups=mesh['shard'=4,'ctx'=2,'tp'=4] {'shard'}, dimensions={0}, use_global_device_ids=true | all-gather | bytes 3840 | tf_op jit(solution)/shard_map/all_gather | solution.py:107
  23.4 1.3 convert_reduce_fusion
  24.7 1.5 fusion.12
  26.3 11.9 %all-gather.1 = bf16[4,192,4]{1,2,0:T(4,128)(2,1)S(1)} all-gather(bf16[1,192,4]{1,2,0:T(4,128)(2,1)S(1)} %bitcast.182), channel_id=1, replica_groups=mesh['shard'=4,'ctx'=2,'tp'=4] {'shard'}, dimensions={0}, use_global_device_ids=true | all-gather | bytes 7680 | tf_op jit(solution)/shard_map/all_gather | solution.py:108
  38.4 15.8 %all_gather.29 = bf16[192,768]{0,1:T(8,128)(2,1)} all-gather(bf16[192,192]{0,1:T(8,128)(2,1)S(1)} %copy.48), channel_id=1, replica_groups=mesh['shard'=4,'ctx'=2,'tp'=4] {'shard'}, dimensions={1}, use_global_device_ids=true | all-gather | bytes 368640 | tf_op jit(solution)/shard_map/all_gather | solution.py:104
  54.5 22.9 %all_gather.26 = bf16[3,768,192]{2,0,1:T(4,128)(2,1)S(1)} all-gather(bf16[3,192,192]{2,0,1:T(4,128)(2,1)S(1)} %copy.42), channel_id=1, replica_groups=mesh['shard'=4,'ctx'=2,'tp'=4] {'shard'}, dimensions={1}, use_global_device_ids=true | all-gather | bytes 1105920 | tf_op jit(solution)/shard_map/all_gather | solution.py:103
  81.4 11.9 %all_gather.28 = bf16[1,1040,192]{2,0,1:T(2,128)(2,1)S(1)} all-gather(bf16[1,520,192]{2,0,1:T(2,128)(2,1)S(1)} %copy.46), channel_id=1, replica_groups=mesh['shard'=4,'ctx'=2,'tp'=4] {'ctx'}, dimensions={1}, use_global_device_ids=true | all-gather | bytes 599040 | tf_op jit(solution)/shard_map/all_gather | solution.py:129
  93.3 2.6 copy.47
  95.9 1.8 copy.44
  97.7 9.9 %all_gather.27 = bf16[1,1040,192]{2,0,1:T(2,128)(2,1)S(1)} all-gather(bf16[1,520,192]{2,0,1:T(2,128)(2,1)S(1)} %copy.44), channel_id=1, replica_groups=mesh['shard'=4,'ctx'=2,'tp'=4] {'ctx'}, dimensions={1}, use_global_device_ids=true | all-gather | bytes 599040 | tf_op jit(solution)/shard_map/all_gather | solution.py:130
  107.7 2.6 copy.45
  110.3 1.5 fusion.56
  111.9 1.4 exponential_reduce_fusion
  113.2 1.6 copy-done
  114.8 1.4 convolution_convert_fusion.2
  116.2 1.6 fusion.57
  120.6 39.9 %all-reduce.9.cloned.1.call-done = f32[520,768]{1,0:T(8,128)} async-done(((f32[520,768]{1,0:T(8,128)}), f32[520,768]{1,0:T(8,128)}) %all-reduce.9.cloned.1.call-update) | async-done | bytes 1597456 | tf_op jit(solution)/shard_map/psum | solution.py:135
  160.5 1.7 fusion.53
  162.6 6.9 %multiply_convert_fusion.1 = (bf16[520,768]{1,0:T(8,128)(2,1)}, f32[520,768]{1,0:T(8,128)}, f32[520,768]{1,0:T(8,128)}) fusion(f32[768]{0:T(1024)S(1)} %convert_element_type.113, bf16[768,768]{1,0:T(8,128)(2,1)} %all-gather.5.cloned.1.call-done, f32[520,768]{1,0:T(8,128)S(1)} %get-tuple-element.132, f32[768]{0:T(1024)S(1)} %get-tuple-element.110, ...), kind=kOutput, calls=%fused_computation.36 | convolution fusion | flops 641771520 | bytes 6784064 | tf_op jit(solution)/shard_map/dot_general | solution.py:140
  169.6 10.6 %all-gather.7.cloned.1.call-done = bf16[768,768]{0,1:T(8,128)(2,1)} async-done(((bf16[768,192]{0,1:T(8,128)(2,1)}), bf16[768,768]{0,1:T(8,128)(2,1)}) %all-gather.7.cloned.1.call-update) | async-done | bytes 1179664 | tf_op jit(solution)/shard_map/all_gather | solution.py:106
  180.2 3.8 convert_reduce_fusion.1
  184.9 2.0 fusion.58
  186.9 42.7 %all-reduce.13.cloned.1.call-done = f32[520,768]{1,0:T(8,128)} async-done(((f32[520,768]{1,0:T(8,128)}), f32[520,768]{1,0:T(8,128)}) %all-reduce.13.cloned.1.call-update) | async-done | bytes 1597456 | tf_op jit(solution)/shard_map/psum | solution.py:166
  229.6 2.3 multiply_reduce_fusion.1
  231.9 2.2 fusion.51
  234.6 1.1 copy-done.3
  236.3 2.5 fusion.24
  238.8 4.8 multiply_reduce_fusion
  243.6 3.7 copy.53
  247.3 2.3 copy.68
  249.7 6.0 %multiply_convert_fusion = bf16[3,520,1040]{2,1,0:T(8,128)(2,1)S(1)} fusion(f32[3,520,1040]{2,1,0:T(8,128)} %get-tuple-element.140, f32[3,520,1040]{2,1,0:T(8,128)} %copy-done, f32[3,520]{1,0:T(4,128)S(1)} %get-tuple-element.139, f32[3,520]{1,0:T(4,128)S(1)} %log_add_fusion), kind=kLoop, calls=%fused_computation | loop fusion | flops 6489600 | bytes 16236480 | tf_op jit(solution)/shard_map/while/body/eval_jaxpr/convert_element_type | solution.py:63
  255.7 2.1 convolution_multiply_fusion
  257.8 3.3 copy.51
  261.1 1.0 copy.69
  262.4 3.4 fusion.23
  265.8 4.5 reduce-scatter.27.cloned.1.call-done
  270.3 1.4 reshape_bitcast_fusion
  272.6 20.4 %reduce-scatter.25.cloned.1.call-done = f32[520,192]{1,0:T(8,128)} async-done(((f32[1040,192]{1,0:T(8,128)}), f32[520,192]{1,0:T(8,128)}) %reduce-scatter.25.cloned.1.call-update) | async-done | bytes 399376
  293.0 1.4 reshape_bitcast_fusion.1
  294.4 1.4 copy.52
  295.8 3.4 convolution_bitcast_fusion.1
  300.2 2.9 convolution_bitcast_fusion.2
  303.1 2.4 convolution_bitcast_fusion
  305.5 4.2 copy.55
  309.7 4.7 reshape.243
  314.6 4.1 fusion.48
  318.7 4.1 fusion.39
  322.8 3.2 convolution_convert_fusion
  326.2 16.6 %all-reduce.15.cloned.1.call-done = f32[520,768]{1,0:T(8,128)} async-done(((f32[520,768]{1,0:T(8,128)}), f32[520,768]{1,0:T(8,128)}) %all-reduce.15.cloned.1.call-update) | async-done | bytes 1597456 | tf_op jit(solution)/shard_map/psum | solution.py:197
  342.8 2.2 fusion.11
  347.1 1.7 copy.58
  348.8 20.7 %reduce-scatter.29.cloned.1.call-done = f32[192,576]{1,0:T(8,128)} async-done(((f32[768,576]{1,0:T(8,128)}), f32[192,576]{1,0:T(8,128)}) %reduce-scatter.29.cloned.1.call-update) | async-done | bytes 442384
  369.5 1.4 reshape.244
  370.9 1.1 copy.56
  372.0 46.6 %reduce-scatter.21.cloned.1.call-done = f32[192,768]{1,0:T(8,128)} async-done(((f32[768,768]{1,0:T(8,128)}), f32[192,768]{1,0:T(8,128)}) %reduce-scatter.21.cloned.1.call-update) | async-done | bytes 589840 | tf_op jit(solution)/shard_map/reduce_scatter | solution.py:221
  418.6 49.6 %reduce-scatter.23.cloned.1.call-done = f32[768,192]{0,1:T(8,128)} async-done(((f32[768,768]{0,1:T(8,128)}), f32[768,192]{0,1:T(8,128)}) %reduce-scatter.23.cloned.1.call-update) | async-done | bytes 589840 | tf_op jit(solution)/shard_map/reduce_scatter | solution.py:222
  468.9 1.8 fusion.31
  471.0 21.1 %all-reduce = (f32[2,192]{1,0:T(2,128)}, f32[768]{0:T(1024)}) all-reduce(f32[2,192]{1,0:T(2,128)S(1)} %pad_maximum_fusion.3, f32[768]{0:T(1024)S(1)} %get-tuple-element.141), channel_id=1, replica_groups=mesh['shard'=4,'ctx'=2,'tp'=4] {'shard','ctx'}, use_global_device_ids=true, to_apply=%region_38.39 | all-reduce | flops 1152 | bytes 9216 | tf_op jit(solution)/shard_map/psum | solution.py:226
  493.0 1.8 fusion.32
  495.8 17.1 %reduce-scatter.35.cloned.1.call-done = f32[192,4]{1,0:T(8,128)} async-done(((f32[768,4]{1,0:T(8,128)}), f32[192,4]{1,0:T(8,128)}) %reduce-scatter.35.cloned.1.call-update) | async-done | bytes 3088
  513.8 5.7 %all-reduce.1 = (f32[2,192]{1,0:T(2,128)}, f32[4,192]{1,0:T(4,128)}) all-reduce(f32[2,192]{1,0:T(2,128)S(1)} %copy.60, f32[4,192]{1,0:T(4,128)S(1)} %copy.62), channel_id=1, replica_groups=mesh['shard'=4,'ctx'=2,'tp'=4] {'ctx'}, use_global_device_ids=true, to_apply=%region_28.29 | all-reduce | flops 1152 | bytes 9216 | tf_op jit(solution)/shard_map/psum | solution.py:217
  519.5 10.2 %all-reduce.17.cloned.1.call-done = (f32[3,192,192]{1,2,0:T(8,128)}, f32[192,192]{1,0:T(8,128)}, f32[192,768]{1,0:T(8,128)}, f32[768,192]{0,1:T(8,128)}) async-done(((f32[3,192,192]{1,2,0:T(8,128)}, f32[192,192]{1,0:T(8,128)}, f32[192,768]{1,0:T(8,128)}, f32[768,192]{0,1:T(8,128)}), (f32[3,192,192]{1,2,0:T(8,128)}, f32[192,192]{1,0:T(8,128)}, f32[192,768]{1,0:T(8,128)}, ...) | async-done | bytes 1769488 | tf_op jit(solution)/shard_map/psum | solution.py:217
  529.8 2.2 copy.50
  532.0 1.6 copy.78
  (142 shorter events, 21.8 us)
Async XLA Ops:
  8.0 18.3 %copy-start.20 = (bf16[4,192]{1,0:T(4,128)(2,1)S(1)}, bf16[4,192]{1,0:T(4,128)(2,1)}, u32[]{:S(2)}) copy-start(bf16[4,192]{1,0:T(4,128)(2,1)} %param.18) | copy-start | bytes 4612
  8.0 30.3 %copy-start.19 = (bf16[192,192]{1,0:T(8,128)(2,1)S(1)}, bf16[192,192]{1,0:T(8,128)(2,1)}, u32[]{:S(2)}) copy-start(bf16[192,192]{1,0:T(8,128)(2,1)} %param.14) | copy-start | bytes 221188
  8.0 46.2 %copy-start.18 = (bf16[3,192,192]{2,1,0:T(8,128)(2,1)S(1)}, bf16[3,192,192]{2,1,0:T(8,128)(2,1)}, u32[]{:S(2)}) copy-start(bf16[3,192,192]{2,1,0:T(8,128)(2,1)} %param.13) | copy-start | bytes 663556
  8.0 152.5 %all-reduce.9.cloned.1.call-start = ((), (), s32[]{:S(2)}) async-start(), calls=%async_computation.8 | async-start | bytes 3194880 | tf_op jit(solution)/shard_map/psum | solution.py:135
  77.4 1.1 copy-start.2
  78.3 1.3 copy-start.14
  95.9 14.4 %copy-start.5 = (bf16[1,1040,192]{1,2,0:T(8,128)(2,1)}, bf16[1,1040,192]{1,2,0:T(8,128)(2,1)S(1)}, u32[]{:S(2)}) copy-start(bf16[1,1040,192]{1,2,0:T(8,128)(2,1)S(1)} %copy.47) | copy-start | bytes 1198084
  111.9 3.0 copy-start
  114.8 1.4 copy-start.6
  116.2 1.7 copy-start.8
  117.9 1.4 copy-start.22
  117.9 2.7 copy-start.21
  117.9 44.7 %all-gather.5.cloned.1.call-start = ((), (), s32[]{:S(2)}) async-start(), calls=%async_computation.9 | async-start | bytes 1474560 | tf_op jit(solution)/shard_map/all_gather | solution.py:105
  118.5 61.7 %all-gather.7.cloned.1.call-start = ((), (), s32[]{:S(2)}) async-start(), calls=%async_computation.10 | async-start | bytes 1474560 | tf_op jit(solution)/shard_map/all_gather | solution.py:106
  119.1 110.5 %all-reduce.13.cloned.1.call-start = ((), (), s32[]{:S(2)}) async-start(), calls=%async_computation.12 | async-start | bytes 3194880 | tf_op jit(solution)/shard_map/psum | solution.py:166
  180.2 4.7 copy-start.23
  184.0 0.9 copy-start.24
  186.9 83.4 %reduce-scatter.27.cloned.1.call-start = ((), (), s32[]{:S(2)}) async-start(), calls=%async_computation.17 | async-start | bytes 1597440
  229.6 6.7 %slice-start = ((s8[7188480]{0:T(1024)(128)(4,1)}), s8[4194304]{0:T(1024)(128)(4,1)S(1)}, s32[]{:S(2)}) async-start(s8[7188480]{0:T(1024)(128)(4,1)} %bitcast.146), calls=%async_computation.23 | async-start | bytes 8388608
  231.9 2.3 copy-start.15
  231.9 4.4 slice-start.1
  234.1 1.6 copy-start.7
  234.6 1.2 copy-start.3
  249.7 43.4 %reduce-scatter.25.cloned.1.call-start = ((), (), s32[]{:S(2)}) async-start(), calls=%async_computation.16 | async-start | bytes 1597440
  255.7 2.1 copy-start.1
  262.1 80.6 %all-reduce.15.cloned.1.call-start = ((), (), s32[]{:S(2)}) async-start(), calls=%async_computation.13 | async-start | bytes 3194880 | tf_op jit(solution)/shard_map/psum | solution.py:197
  272.6 30.5 %copy-start.10 = (bf16[1,520,192]{1,2,0:T(8,128)(2,1)}, bf16[1,520,192]{1,2,0:T(8,128)(2,1)S(1)}, u32[]{:S(2)}) copy-start(bf16[1,520,192]{1,2,0:T(8,128)(2,1)S(1)} %copy.54) | copy-start | bytes 599044
  299.2 0.9 copy-start.9
  299.2 3.9 copy-start.12
  299.2 47.8 %reduce-scatter.31.cloned.1.call-start = ((), (), s32[]{:S(2)}) async-start(), calls=%async_computation.19 | async-start | bytes 983040
  303.0 66.4 %reduce-scatter.29.cloned.1.call-start = ((), (), s32[]{:S(2)}) async-start(), calls=%async_computation.18 | async-start | bytes 2457600
  314.5 104.1 %reduce-scatter.21.cloned.1.call-start = ((), (), s32[]{:S(2)}) async-start(), calls=%async_computation.14 | async-start | bytes 2949120 | tf_op jit(solution)/shard_map/reduce_scatter | solution.py:221
  318.6 149.6 %reduce-scatter.23.cloned.1.call-start = ((), (), s32[]{:S(2)}) async-start(), calls=%async_computation.15 | async-start | bytes 2949120 | tf_op jit(solution)/shard_map/reduce_scatter | solution.py:222
  322.8 146.1 %all-reduce.11.cloned.1.call-start = ((), (), s32[]{:S(2)}) async-start(), calls=%async_computation.11 | async-start | bytes 1597440 | tf_op jit(solution)/shard_map/psum | solution.py:146
  326.1 168.7 %reduce-scatter.33.cloned.1.call-start = ((), (), s32[]{:S(2)}) async-start(), calls=%async_computation.20 | async-start | bytes 491520
  346.0 166.9 %reduce-scatter.35.cloned.1.call-start = ((), (), s32[]{:S(2)}) async-start(), calls=%async_computation.21 | async-start | bytes 491520
  347.0 182.7 %all-reduce.17.cloned.1.call-start = ((), (), s32[]{:S(2)}) async-start(), calls=%async_computation.22 | async-start | bytes 3932160 | tf_op jit(solution)/shard_map/psum | solution.py:217
  372.0 98.7 %copy-start.11 = (bf16[1,520,192]{1,2,0:T(8,128)(2,1)S(1)}, bf16[1,520,192]{1,2,0:T(8,128)(2,1)}, u32[]{:S(2)}) copy-start(bf16[1,520,192]{1,2,0:T(8,128)(2,1)} %copy-done.10) | copy-start | bytes 599044
  372.0 98.7 %copy-start.13 = (bf16[1,520,192]{1,2,0:T(8,128)(2,1)S(1)}, bf16[1,520,192]{1,2,0:T(8,128)(2,1)}, u32[]{:S(2)}) copy-start(bf16[1,520,192]{1,2,0:T(8,128)(2,1)} %copy.52) | copy-start | bytes 599044
  470.7 21.5 %copy-start.4 = (f32[520,768]{1,0:T(8,128)S(1)}, f32[520,768]{1,0:T(8,128)}, u32[]{:S(2)}) copy-start(f32[520,768]{1,0:T(8,128)} %all-reduce.15.cloned.1.call-done) | copy-start | bytes 4792324
  529.7 3.8 copy-start.17
  529.8 4.7 copy-start.16
Sparse Core Ops, SparseCore 0:
  118.0 42.4 all-reduce.8
  187.0 42.5 all-reduce.12
  249.8 20.4 reduce-scatter.26
  272.5 20.4 reduce-scatter.24
  299.4 43.3 all-reduce.14
  345.0 34.5 all-reduce.10
  468.3 61.3 all-reduce.16
Sparse Core Ops, SparseCore 1:
  120.0 29.3 all-gather.4
  150.7 29.4 all-gather.6
  303.1 23.0 reduce-scatter.30
  328.5 40.9 reduce-scatter.28
  371.8 46.7 reduce-scatter.20
  420.9 47.2 reduce-scatter.22
  471.0 20.1 reduce-scatter.32
  493.9 18.9 reduce-scatter.34
where the time goes:
time: 544 us; the launch traced here: 543 us
  waiting for transfers between devices  280 us (51%)
  blocking collectives  112 us (21%)
  local copies, waits for them, and re-layouts  53.1 us (10%)
  matrix products  51.7 us (10%)
  other arithmetic  28.1 us (5%)
  between operations  16.2 us (3%)
    unnamed x21, waiting for transfers between devices  63.9 us
    reduce_scatter x1, waiting for transfers between devices, per_device(): lax.psum_scatter(summed[3], 'shard', scatter_dimension=1, tiled=True)  49.6 us
    reduce_scatter x1, waiting for transfers between devices, per_device(): lax.psum_scatter(summed[2], 'shard', scatter_dimension=0, tiled=True)  46.6 us
    unnamed x77, local copies, waits for them, and re-layouts  43 us
    psum x1, waiting for transfers between devices, per_device(): grad_normed_two = lax.psum(grad_normed_part, 'tp')  42.7 us
    psum x1, waiting for transfers between devices, per_device(): attn_sum = lax.psum(attn_part, 'tp')  39.9 us
    all_gather x1, blocking collectives, per_device(): lax.all_gather(qkv_weight, 'shard', axis=1, tiled=True)  22.9 us
    psum x1, blocking collectives, per_device(): bias_totals = lax.psum((head_grad, hidden_grad), ('shard', 'ctx'))  21.1 us
  transfers between devices with their start and end apart: 15, of which 11 were waited for; matrix products, arithmetic and copies ran while one was open for 13% of the time, Pallas kernels for 0%

commit v1 on v0

--- a/solution.py
+++ b/solution.py
@@ -7,6 +7,34 @@
 HD = 64
 EPS = 1e-06
 NEG = -1e30
+
+
+def _perform_frame(z_in, d0):
+    z_in = jnp.moveaxis(z_in, 0, d0)
+    current_block = z_in.shape
+    return z_in.reshape(
+        *current_block[:d0], current_block[d0] * current_block[d0 + 1], *current_block[d0 + 2 :]
+    )
+
+
+def arrange_page(sample, a_name, in_dim):
+    cores_n = jax.lax.axis_size(a_name)
+    log = list(map(lambda i0: (i0, (i0 + 1) % cores_n), range(cores_n)))
+    inbox = [(p, tick) for tick, p in log]
+    tile_out, answer = ([], [])
+    for b in tuple(range(cores_n - 1)):
+        if b % 2 == 0:
+            tile_out.append(
+                jax.lax.ppermute(tile_out[-1] if tile_out else sample, axis_name=a_name, perm=log)
+            )
+        else:
+            answer.append(
+                jax.lax.ppermute(answer[-1] if answer else sample, perm=inbox, axis_name=a_name)
+            )
+    finding = jnp.stack([*tile_out[::-1], sample, *answer], axis=0)
+    f_next = jax.lax.axis_index(a_name) - len(tile_out)
+    finding = finding[(jnp.arange(cores_n) - f_next) % cores_n]
+    return _perform_frame(finding, in_dim)
 
 
 def layer_norm(values, gain, shift):
@@ -104,7 +132,7 @@
         lax.all_gather(proj_weight, "shard", axis=1, tiled=True),
         lax.all_gather(up_weight, "shard", axis=0, tiled=True),
         lax.all_gather(down_weight, "shard", axis=1, tiled=True),
-        lax.all_gather(norm_gains, "shard", axis=1, tiled=True),
+        arrange_page(norm_gains, "shard", 1),
         lax.all_gather(row_biases, "shard", axis=1, tiled=True),
     )
     qkv_full, proj_full, up_full, down_full, gains_full, shifts_full = gathered

time: 544 us -> 542 us (level)
  blocking collectives: 112 us -> 102 us
    all_gather x1 -> x0, blocking collectives: 12.8 us -> none  [per_device(): lax.all_gather(norm_gains, 'shard', axis=1, tiled=True)]
    unnamed x77 -> x81, local copies, waits for them, and re-layouts: 43 us -> 42.7 us
  transfers between devices with their start and end apart: 15 -> 18, of which waited for: 11 -> 11; matrix products, arithmetic and copies ran while one was open for 13% -> 14% of each run, Pallas kernels for 0% -> 0%
where the time goes in v1:
time: 542 us; the launch traced here: 540 us
  waiting for transfers between devices  283 us (52%)
  blocking collectives  102 us (19%)
  local copies, waits for them, and re-layouts  52.8 us (10%)
  matrix products  51.7 us (10%)
  other arithmetic  28.2 us (5%)
  between operations  16.3 us (3%)
  starting transfers between devices  6.27 us (1%)
    unnamed x21, waiting for transfers between devices  63.9 us
    reduce_scatter x1, waiting for transfers between devices, per_device(): lax.psum_scatter(summed[3], 'shard', scatter_dimension=1, tiled=True)  49.4 us
    reduce_scatter x1, waiting for transfers between devices, per_device(): lax.psum_scatter(summed[2], 'shard', scatter_dimension=0, tiled=True)  46.8 us
    psum x1, waiting for transfers between devices, per_device(): attn_sum = lax.psum(attn_part, 'tp')  43 us
    unnamed x81, local copies, waits for them, and re-layouts  42.7 us
    psum x1, waiting for transfers between devices, per_device(): grad_normed_two = lax.psum(grad_normed_part, 'tp')  42.7 us
    all_gather x1, blocking collectives, per_device(): lax.all_gather(qkv_weight, 'shard', axis=1, tiled=True)  26.9 us
    psum x1, blocking collectives, per_device(): bias_totals = lax.psum((head_grad, hidden_grad), ('shard', 'ctx'))  21.2 us
  transfers between devices with their start and end apart: 18, of which 11 were waited for; matrix products, arithmetic and copies ran while one was open for 14% of the time, Pallas kernels for 0%

profile of v1, /device:TPU:0, one launch (start us, length us, event | category | flops | bytes accessed | tf_op | source)
XLA Modules:
  0.0 540.4 jit_solution(4045531123295723984)
XLA Ops:
  8.1 3.1 collective-permute-start
  11.2 2.1 collective-permute-start.2
  14.7 1.3 convert_reduce_fusion
  16.0 1.5 fusion.12
  17.6 11.9 %all-gather = bf16[4,192,4]{1,2,0:T(4,128)(2,1)S(1)} all-gather(bf16[1,192,4]{1,2,0:T(4,128)(2,1)S(1)} %bitcast.183), channel_id=1, replica_groups=mesh['shard'=4,'ctx'=2,'tp'=4] {'shard'}, dimensions={0}, use_global_device_ids=true | all-gather | bytes 7680 | tf_op jit(solution)/shard_map/all_gather | solution.py:136
  29.9 26.9 %all_gather.22 = bf16[3,768,192]{2,0,1:T(4,128)(2,1)S(1)} all-gather(bf16[3,192,192]{2,0,1:T(4,128)(2,1)S(1)} %copy.29), channel_id=1, replica_groups=mesh['shard'=4,'ctx'=2,'tp'=4] {'shard'}, dimensions={1}, use_global_device_ids=true | all-gather | bytes 1105920 | tf_op jit(solution)/shard_map/all_gather | solution.py:131
  57.0 15.6 %all_gather.25 = bf16[192,768]{0,1:T(8,128)(2,1)} all-gather(bf16[192,192]{0,1:T(8,128)(2,1)S(1)} %copy.35), channel_id=1, replica_groups=mesh['shard'=4,'ctx'=2,'tp'=4] {'shard'}, dimensions={1}, use_global_device_ids=true | all-gather | bytes 368640 | tf_op jit(solution)/shard_map/all_gather | solution.py:132
  77.3 10.8 %all_gather.24 = bf16[1,1040,192]{2,0,1:T(2,128)(2,1)S(1)} all-gather(bf16[1,520,192]{2,0,1:T(2,128)(2,1)S(1)} %copy.33), channel_id=1, replica_groups=mesh['shard'=4,'ctx'=2,'tp'=4] {'ctx'}, dimensions={1}, use_global_device_ids=true | all-gather | bytes 599040 | tf_op jit(solution)/shard_map/all_gather | solution.py:157
  88.0 2.6 copy.34
  90.7 1.8 copy.31
  92.5 9.9 %all_gather.23 = bf16[1,1040,192]{2,0,1:T(2,128)(2,1)S(1)} all-gather(bf16[1,520,192]{2,0,1:T(2,128)(2,1)S(1)} %copy.31), channel_id=1, replica_groups=mesh['shard'=4,'ctx'=2,'tp'=4] {'ctx'}, dimensions={1}, use_global_device_ids=true | all-gather | bytes 599040 | tf_op jit(solution)/shard_map/all_gather | solution.py:158
  102.5 2.6 copy.32
  105.1 1.5 fusion.58
  106.6 1.4 exponential_reduce_fusion
  108.0 1.6 copy-done
  109.6 1.4 convolution_convert_fusion.2
  111.0 1.6 fusion.59
  115.5 43.0 %all-reduce.9.cloned.1.call-done = f32[520,768]{1,0:T(8,128)} async-done(((f32[520,768]{1,0:T(8,128)}), f32[520,768]{1,0:T(8,128)}) %all-reduce.9.cloned.1.call-update) | async-done | bytes 1597456 | tf_op jit(solution)/shard_map/psum | solution.py:163
  158.5 1.7 fusion.55
  160.6 6.9 %multiply_convert_fusion.1 = (bf16[520,768]{1,0:T(8,128)(2,1)}, f32[520,768]{1,0:T(8,128)}, f32[520,768]{1,0:T(8,128)}) fusion(f32[768]{0:T(1024)S(1)} %convert_element_type.118, bf16[768,768]{1,0:T(8,128)(2,1)} %all-gather.4.cloned.1.call-done, f32[520,768]{1,0:T(8,128)S(1)} %get-tuple-element.122, f32[768]{0:T(1024)S(1)} %get-tuple-element.100, ...), kind=kOutput, calls=%fused_computation.37 | convolution fusion | flops 641771520 | bytes 6784064 | tf_op jit(solution)/shard_map/dot_general | solution.py:168
  167.5 10.6 %all-gather.6.cloned.1.call-done = bf16[768,768]{0,1:T(8,128)(2,1)} async-done(((bf16[768,192]{0,1:T(8,128)(2,1)}), bf16[768,768]{0,1:T(8,128)(2,1)}) %all-gather.6.cloned.1.call-update) | async-done | bytes 1179664 | tf_op jit(solution)/shard_map/all_gather | solution.py:134
  178.1 3.8 convert_reduce_fusion.1
  182.8 2.0 fusion.60
  184.9 42.7 %all-reduce.13.cloned.1.call-done = f32[520,768]{1,0:T(8,128)} async-done(((f32[520,768]{1,0:T(8,128)}), f32[520,768]{1,0:T(8,128)}) %all-reduce.13.cloned.1.call-update) | async-done | bytes 1597456 | tf_op jit(solution)/shard_map/psum | solution.py:194
  227.5 2.3 multiply_reduce_fusion.1
  229.8 2.2 fusion.53
  232.5 1.1 copy-done.3
  234.2 2.5 fusion.24
  236.8 4.8 multiply_reduce_fusion
  241.6 3.7 copy.40
  245.3 2.3 copy.54
  247.6 6.0 %multiply_convert_fusion = bf16[3,520,1040]{2,1,0:T(8,128)(2,1)S(1)} fusion(f32[3,520,1040]{2,1,0:T(8,128)} %get-tuple-element.130, f32[3,520,1040]{2,1,0:T(8,128)} %copy-done, f32[3,520]{1,0:T(4,128)S(1)} %get-tuple-element.129, f32[3,520]{1,0:T(4,128)S(1)} %log_add_fusion), kind=kLoop, calls=%fused_computation.1 | loop fusion | flops 6489600 | bytes 16236480 | tf_op jit(solution)/shard_map/while/body/eval_jaxpr/convert_element_type | solution.py:91
  253.6 2.1 convolution_multiply_fusion
  255.7 3.3 copy.38
  260.3 3.4 fusion.23
  263.7 4.5 reduce-scatter.27.cloned.1.call-done
  268.2 1.4 reshape_bitcast_fusion
  270.5 20.4 %reduce-scatter.25.cloned.1.call-done = f32[520,192]{1,0:T(8,128)} async-done(((f32[1040,192]{1,0:T(8,128)}), f32[520,192]{1,0:T(8,128)}) %reduce-scatter.25.cloned.1.call-update) | async-done | bytes 399376
  291.0 1.4 reshape_bitcast_fusion.1
  292.4 1.4 copy.39
  293.7 3.4 convolution_bitcast_fusion.1
  298.1 2.9 convolution_bitcast_fusion.2
  301.1 2.4 convolution_bitcast_fusion
  303.5 4.2 copy.42
  307.7 4.7 reshape.303
  312.5 4.0 fusion.50
  316.6 4.1 fusion.41
  320.8 3.2 convolution_convert_fusion
  324.1 16.6 %all-reduce.15.cloned.1.call-done = f32[520,768]{1,0:T(8,128)} async-done(((f32[520,768]{1,0:T(8,128)}), f32[520,768]{1,0:T(8,128)}) %all-reduce.15.cloned.1.call-update) | async-done | bytes 1597456 | tf_op jit(solution)/shard_map/psum | solution.py:225
  340.7 2.2 fusion.11
  345.0 1.7 copy.45
  346.7 20.7 %reduce-scatter.29.cloned.1.call-done = f32[192,576]{1,0:T(8,128)} async-done(((f32[768,576]{1,0:T(8,128)}), f32[192,576]{1,0:T(8,128)}) %reduce-scatter.29.cloned.1.call-update) | async-done | bytes 442384
  367.4 1.4 reshape.304
  368.8 1.1 copy.43
  369.9 46.8 %reduce-scatter.21.cloned.1.call-done = f32[192,768]{1,0:T(8,128)} async-done(((f32[768,768]{1,0:T(8,128)}), f32[192,768]{1,0:T(8,128)}) %reduce-scatter.21.cloned.1.call-update) | async-done | bytes 589840 | tf_op jit(solution)/shard_map/reduce_scatter | solution.py:249
  416.7 49.4 %reduce-scatter.23.cloned.1.call-done = f32[768,192]{0,1:T(8,128)} async-done(((f32[768,768]{0,1:T(8,128)}), f32[768,192]{0,1:T(8,128)}) %reduce-scatter.23.cloned.1.call-update) | async-done | bytes 589840 | tf_op jit(solution)/shard_map/reduce_scatter | solution.py:250
  466.7 1.8 fusion.31
  468.8 21.2 %all-reduce = (f32[2,192]{1,0:T(2,128)}, f32[768]{0:T(1024)}) all-reduce(f32[2,192]{1,0:T(2,128)S(1)} %pad_maximum_fusion.4, f32[768]{0:T(1024)S(1)} %get-tuple-element.131), channel_id=1, replica_groups=mesh['shard'=4,'ctx'=2,'tp'=4] {'shard','ctx'}, use_global_device_ids=true, to_apply=%region_38.39 | all-reduce | flops 1152 | bytes 9216 | tf_op jit(solution)/shard_map/psum | solution.py:254
  490.8 1.8 fusion.32
  493.6 17.0 %reduce-scatter.35.cloned.1.call-done = f32[192,4]{1,0:T(8,128)} async-done(((f32[768,4]{1,0:T(8,128)}), f32[192,4]{1,0:T(8,128)}) %reduce-scatter.35.cloned.1.call-update) | async-done | bytes 3088
  511.6 5.7 %all-reduce.1 = (f32[2,192]{1,0:T(2,128)}, f32[4,192]{1,0:T(4,128)}) all-reduce(f32[2,192]{1,0:T(2,128)S(1)} %copy.47, f32[4,192]{1,0:T(4,128)S(1)} %copy.49), channel_id=1, replica_groups=mesh['shard'=4,'ctx'=2,'tp'=4] {'ctx'}, use_global_device_ids=true, to_apply=%region_28.29 | all-reduce | flops 1152 | bytes 9216 | tf_op jit(solution)/shard_map/psum | solution.py:245
  517.3 10.2 %all-reduce.17.cloned.1.call-done = (f32[3,192,192]{1,2,0:T(8,128)}, f32[192,192]{1,0:T(8,128)}, f32[192,768]{1,0:T(8,128)}, f32[768,192]{0,1:T(8,128)}) async-done(((f32[3,192,192]{1,2,0:T(8,128)}, f32[192,192]{1,0:T(8,128)}, f32[192,768]{1,0:T(8,128)}, f32[768,192]{0,1:T(8,128)}), (f32[3,192,192]{1,2,0:T(8,128)}, f32[192,192]{1,0:T(8,128)}, f32[192,768]{1,0:T(8,128)}, ...) | async-done | bytes 1769488 | tf_op jit(solution)/shard_map/psum | solution.py:245
  527.5 2.2 copy.37
  529.7 1.6 copy.64
  (156 shorter events, 22.6 us)
Async XLA Ops:
  8.0 9.6 %copy-start.21 = (bf16[4,192]{1,0:T(4,128)(2,1)S(1)}, bf16[4,192]{1,0:T(4,128)(2,1)}, u32[]{:S(2)}) copy-start(bf16[4,192]{1,0:T(4,128)(2,1)} %param.18) | copy-start | bytes 4612
  8.0 21.6 %copy-start.18 = (bf16[3,192,192]{2,1,0:T(8,128)(2,1)S(1)}, bf16[3,192,192]{2,1,0:T(8,128)(2,1)}, u32[]{:S(2)}) copy-start(bf16[3,192,192]{2,1,0:T(8,128)(2,1)} %param.13) | copy-start | bytes 663556
  8.0 150.5 %all-reduce.9.cloned.1.call-start = ((), (), s32[]{:S(2)}) async-start(), calls=%async_computation.8 | async-start | bytes 3194880 | tf_op jit(solution)/shard_map/psum | solution.py:163
  8.1 48.9 %collective-permute-start = (bf16[2,192]{1,0:T(2,128)(2,1)}, bf16[2,192]{1,0:T(2,128)(2,1)S(1)}, u32[]{:S(2)}, u32[]{:S(2)}) collective-permute-start(bf16[2,192]{1,0:T(2,128)(2,1)} %param.17), channel_id=1, source_target_pairs={{0,8},{8,16},{16,24},{24,0},{1,9},{9,17},{17,25},{25,1},{2,10},{10... | collective-permute-start | bytes 2312 | tf_op jit(solution)/shard_map/ppermute | solution.py:28
  11.2 62.6 %collective-permute-start.2 = (bf16[2,192]{1,0:T(2,128)(2,1)}, bf16[2,192]{1,0:T(2,128)(2,1)S(1)}, u32[]{:S(2)}, u32[]{:S(2)}) collective-permute-start(bf16[2,192]{1,0:T(2,128)(2,1)} %param.17), channel_id=1, source_target_pairs={{8,0},{16,8},{24,16},{0,24},{9,1},{17,9},{25,17},{1,25},{10,2},{18... | collective-permute-start | bytes 2312 | tf_op jit(solution)/shard_map/ppermute | solution.py:32
  16.0 40.8 %copy-start.19 = (bf16[192,192]{1,0:T(8,128)(2,1)S(1)}, bf16[192,192]{1,0:T(8,128)(2,1)}, u32[]{:S(2)}) copy-start(bf16[192,192]{1,0:T(8,128)(2,1)} %param.14) | copy-start | bytes 221188
  29.6 43.0 %copy-start.20 = (bf16[2,192]{1,0:T(2,128)(2,1)S(1)}, bf16[2,192]{1,0:T(2,128)(2,1)}, u32[]{:S(2)}) copy-start(bf16[2,192]{1,0:T(2,128)(2,1)} %param.19) | copy-start | bytes 2308
  56.8 17.0 %copy-start.23 = (bf16[2,192]{1,0:T(2,128)(2,1)S(1)}, bf16[2,192]{1,0:T(2,128)(2,1)}, u32[]{:S(2)}) copy-start(bf16[2,192]{1,0:T(2,128)(2,1)} %param.17) | copy-start | bytes 2308
  56.8 17.7 %copy-start.2 = (bf16[1,520,768]{2,1,0:T(8,128)(2,1)S(1)}, bf16[1,520,768]{2,1,0:T(8,128)(2,1)}, u32[]{:S(2)}) copy-start(bf16[1,520,768]{2,1,0:T(8,128)(2,1)} %param.11) | copy-start | bytes 2396164
  56.9 16.8 %collective-permute-start.1 = (bf16[2,192]{1,0:T(2,128)(2,1)S(1)}, bf16[2,192]{1,0:T(2,128)(2,1)S(1)}, u32[]{:S(2)}, u32[]{:S(2)}) collective-permute-start(bf16[2,192]{1,0:T(2,128)(2,1)S(1)} %collective-permute-done), channel_id=1, source_target_pairs={{0,8},{8,16},{16,24},{24,0},{1,9},{9,17},{17,25},{25,1},{2,10},{10... | collective-permute-start | bytes 2312 | tf_op jit(solution)/shard_map/ppermute | solution.py:28
  73.7 1.8 copy-start.14
  90.7 14.4 %copy-start.5 = (bf16[1,1040,192]{1,2,0:T(8,128)(2,1)}, bf16[1,1040,192]{1,2,0:T(8,128)(2,1)S(1)}, u32[]{:S(2)}) copy-start(bf16[1,1040,192]{1,2,0:T(8,128)(2,1)S(1)} %copy.34) | copy-start | bytes 1198084
  106.6 3.0 copy-start
  109.6 1.4 copy-start.6
  111.0 1.7 copy-start.8
  112.7 1.4 copy-start.24
  112.7 2.7 copy-start.22
  112.7 47.9 %all-gather.4.cloned.1.call-start = ((), (), s32[]{:S(2)}) async-start(), calls=%async_computation.9 | async-start | bytes 1474560 | tf_op jit(solution)/shard_map/all_gather | solution.py:133
  113.3 64.8 %all-gather.6.cloned.1.call-start = ((), (), s32[]{:S(2)}) async-start(), calls=%async_computation.10 | async-start | bytes 1474560 | tf_op jit(solution)/shard_map/all_gather | solution.py:134
  113.9 113.7 %all-reduce.13.cloned.1.call-start = ((), (), s32[]{:S(2)}) async-start(), calls=%async_computation.12 | async-start | bytes 3194880 | tf_op jit(solution)/shard_map/psum | solution.py:194
  178.1 4.7 copy-start.25
  181.9 0.9 copy-start.26
  184.8 83.4 %reduce-scatter.27.cloned.1.call-start = ((), (), s32[]{:S(2)}) async-start(), calls=%async_computation.17 | async-start | bytes 1597440
  227.5 6.7 %slice-start = ((s8[7188480]{0:T(1024)(128)(4,1)}), s8[4194304]{0:T(1024)(128)(4,1)S(1)}, s32[]{:S(2)}) async-start(s8[7188480]{0:T(1024)(128)(4,1)} %bitcast.148), calls=%async_computation.23 | async-start | bytes 8388608
  229.8 2.3 copy-start.15
  229.8 4.4 slice-start.1
  232.1 1.6 copy-start.7
  232.5 1.2 copy-start.3
  247.6 43.4 %reduce-scatter.25.cloned.1.call-start = ((), (), s32[]{:S(2)}) async-start(), calls=%async_computation.16 | async-start | bytes 1597440
  253.6 2.1 copy-start.1
  260.1 80.6 %all-reduce.15.cloned.1.call-start = ((), (), s32[]{:S(2)}) async-start(), calls=%async_computation.13 | async-start | bytes 3194880 | tf_op jit(solution)/shard_map/psum | solution.py:225
  270.5 30.5 %copy-start.10 = (bf16[1,520,192]{1,2,0:T(8,128)(2,1)}, bf16[1,520,192]{1,2,0:T(8,128)(2,1)S(1)}, u32[]{:S(2)}) copy-start(bf16[1,520,192]{1,2,0:T(8,128)(2,1)S(1)} %copy.41) | copy-start | bytes 599044
  297.1 0.9 copy-start.9
  297.2 3.9 copy-start.12
  297.2 47.8 %reduce-scatter.31.cloned.1.call-start = ((), (), s32[]{:S(2)}) async-start(), calls=%async_computation.19 | async-start | bytes 983040
  301.0 66.4 %reduce-scatter.29.cloned.1.call-start = ((), (), s32[]{:S(2)}) async-start(), calls=%async_computation.18 | async-start | bytes 2457600
  312.4 104.2 %reduce-scatter.21.cloned.1.call-start = ((), (), s32[]{:S(2)}) async-start(), calls=%async_computation.14 | async-start | bytes 2949120 | tf_op jit(solution)/shard_map/reduce_scatter | solution.py:249
  316.6 149.5 %reduce-scatter.23.cloned.1.call-start = ((), (), s32[]{:S(2)}) async-start(), calls=%async_computation.15 | async-start | bytes 2949120 | tf_op jit(solution)/shard_map/reduce_scatter | solution.py:250
  320.7 146.0 %all-reduce.11.cloned.1.call-start = ((), (), s32[]{:S(2)}) async-start(), calls=%async_computation.11 | async-start | bytes 1597440 | tf_op jit(solution)/shard_map/psum | solution.py:174
  324.0 168.6 %reduce-scatter.33.cloned.1.call-start = ((), (), s32[]{:S(2)}) async-start(), calls=%async_computation.20 | async-start | bytes 491520
  343.9 166.7 %reduce-scatter.35.cloned.1.call-start = ((), (), s32[]{:S(2)}) async-start(), calls=%async_computation.21 | async-start | bytes 491520
  344.9 182.5 %all-reduce.17.cloned.1.call-start = ((), (), s32[]{:S(2)}) async-start(), calls=%async_computation.22 | async-start | bytes 3932160 | tf_op jit(solution)/shard_map/psum | solution.py:245
  369.9 98.6 %copy-start.11 = (bf16[1,520,192]{1,2,0:T(8,128)(2,1)S(1)}, bf16[1,520,192]{1,2,0:T(8,128)(2,1)}, u32[]{:S(2)}) copy-start(bf16[1,520,192]{1,2,0:T(8,128)(2,1)} %copy-done.10) | copy-start | bytes 599044
  369.9 98.6 %copy-start.13 = (bf16[1,520,192]{1,2,0:T(8,128)(2,1)S(1)}, bf16[1,520,192]{1,2,0:T(8,128)(2,1)}, u32[]{:S(2)}) copy-start(bf16[1,520,192]{1,2,0:T(8,128)(2,1)} %copy.39) | copy-start | bytes 599044
  468.5 21.5 %copy-start.4 = (f32[520,768]{1,0:T(8,128)S(1)}, f32[520,768]{1,0:T(8,128)}, u32[]{:S(2)}) copy-start(f32[520,768]{1,0:T(8,128)} %all-reduce.15.cloned.1.call-done) | copy-start | bytes 4792324
  527.5 3.8 copy-start.17
  527.5 4.7 copy-start.16
Sparse Core Ops, SparseCore 0:
  112.8 45.6 all-reduce.8
  185.0 42.5 all-reduce.12
  247.7 20.4 reduce-scatter.26
  270.4 20.4 reduce-scatter.24
  297.3 43.3 all-reduce.14
  342.9 34.5 all-reduce.10
  466.2 61.2 all-reduce.16
Sparse Core Ops, SparseCore 1:
  114.7 32.5 all-gather.3
  148.7 29.4 all-gather.5
  301.1 23.0 reduce-scatter.30
  326.5 40.9 reduce-scatter.28
  369.7 46.9 reduce-scatter.20
  419.0 47.0 reduce-scatter.22
  468.8 19.8 reduce-scatter.32
  491.4 19.1 reduce-scatter.34
